TPU v7x, 32 devices: a whole 2x2x4 slice. The times are simulated.
32 devices in a mesh: row: 4 (over y, x), col: 8 (over z, core).
Axes of the slice: x: 2, y: 2, z: 4, core: 2. Of those that a mesh axis runs over, the one named last changes fastest.
Arguments:
- node_features: bfloat16 [4096, 1024], P(('row', 'col')), may hold values from -6 to 6
- norm_gain: float32 [1024], replicated, may hold values from 0.5 to 1.5
- w_query: bfloat16 [1024, 1024], replicated, may hold values from -0.1875 to 0.1875
- w_keyvalue: bfloat16 [1024, 2048], replicated, may hold values from -0.1875 to 0.1875
- w_out: bfloat16 [1024, 1024], replicated, may hold values from -0.1875 to 0.1875
- bias_table: float32 [32, 8], replicated, may hold values from -4 to 4
- edge_slope: float32 [8], replicated, may hold values from 0.5 to 1.5
- pair_blocks: int32 [4, 8, 2, 16], P('row', 'col'), may hold values from -1 to 7, as said below
- bucket_ids: int32 [4, 8, 16, 128, 128], P('row', 'col'), may hold values from 0 to 31
- edge_weight: bfloat16 [4, 8, 4, 4, 128, 128], P('row', 'col'), may hold values from -4 to 240
Outputs:
- node_out: bfloat16 [4096, 1024], P(('row', 'col'))
Inputs may be any that keep to these rules, and one draw needn't show every extreme that they name: `pair_blocks`: slots of a tile with query block -1 are empty and name key block 0. The listed pairs of a tile are distinct; each tile (r, c) lists, among the slots from t = r, every block of node shard r * 8 + c paired with itself. Up to 4 slots from one owner to one row range are used, and some tile uses all 16 of its slots.
All inputs are finite; a program needn't handle non-finite values.
Results may differ from a plain program's by a relative error of at most 0.005.
Values may be sent and summed in bfloat16 or wider, within the bound.
A program may use at most 256 MiB of HBM per device.

v0:
```python
import math
import jax
import jax.numpy as jnp
from jax import lax
from jax.sharding import PartitionSpec as P

EPSILON = 1e-05
LOW_FLOOR = -1e30


def normalize(features, gain_vec):
    as_float = features.astype(jnp.float32)
    centered = as_float - jnp.mean(as_float, axis=-1, keepdims=True)
    variance = jnp.mean(centered * centered, axis=-1, keepdims=True)
    return (centered * lax.rsqrt(variance + EPSILON) * gain_vec).astype(jnp.bfloat16)


def local(
    node_features,
    norm_gain,
    w_query,
    w_keyvalue,
    w_out,
    bias_table,
    edge_slope,
    pair_blocks,
    bucket_ids,
    edge_weight,
):
    rows_own, model_width = node_features.shape
    head_count = edge_slope.shape[0]
    head_dim = model_width // head_count
    tile_size = bucket_ids.shape[-1]
    bucket_count = bias_table.shape[0]
    normalized = normalize(node_features, norm_gain)
    queries = jnp.dot(normalized, w_query, preferred_element_type=jnp.float32).astype(jnp.bfloat16)
    query_range = lax.all_gather(queries, "col", axis=0, tiled=True)
    key_value = jnp.dot(normalized, w_keyvalue, preferred_element_type=jnp.float32).astype(
        jnp.bfloat16
    )
    key_group = lax.all_gather(key_value, "row", axis=0, tiled=True)
    arrived = lax.all_to_all(edge_weight, "row", split_axis=2, concat_axis=0, tiled=True)
    slot_count = arrived.shape[0] * arrived.shape[3]
    edge_values = arrived.reshape(slot_count, tile_size, tile_size)
    pair_table = pair_blocks.reshape(2, slot_count)
    bucket_tiles = bucket_ids.reshape(slot_count, tile_size, tile_size)
    query_count = query_range.shape[0] // tile_size
    slot_cap = slot_count // lax.axis_size("row")
    key_blocks = rows_own // tile_size
    query_block = pair_table[0]
    key_block = pair_table[1] + jnp.arange(slot_count, dtype=jnp.int32) // slot_cap * key_blocks
    query_flat = query_range.reshape(query_count, tile_size * model_width)
    key_count = key_group.shape[0] // tile_size
    key_flat = key_group.reshape(key_count, tile_size * 2 * model_width)
    query_ids = jnp.arange(query_count, dtype=jnp.int32)
    key_ids = jnp.arange(key_count, dtype=jnp.int32)
    bucket_range = jnp.arange(bucket_count, dtype=jnp.int32)
    batch_size = math.gcd(slot_count, max(1, 512 // tile_size))
    turn_count = slot_count // batch_size
    score_scale = head_dim ** (-0.5)

    def score_slots(inputs):
        query_index, key_index, tile_weights, tile_buckets = inputs
        query_pick = (jnp.maximum(query_index, 0)[:, None] == query_ids[None, :]).astype(
            jnp.bfloat16
        )
        key_pick = (key_index[:, None] == key_ids[None, :]).astype(jnp.bfloat16)
        query_sel = jnp.dot(query_pick, query_flat, preferred_element_type=jnp.float32).astype(
            jnp.bfloat16
        )
        query_sel = query_sel.reshape(batch_size, tile_size, head_count, head_dim)
        pair_sel = jnp.dot(key_pick, key_flat, preferred_element_type=jnp.float32).astype(
            jnp.bfloat16
        )
        pair_sel = pair_sel.reshape(batch_size, tile_size, 2, head_count, head_dim)
        key_sel = pair_sel[:, :, 0]
        value_sel = pair_sel[:, :, 1]
        raw_score = (
            jnp.einsum("sihd,sjhd->shij", query_sel, key_sel, preferred_element_type=jnp.float32)
            * score_scale
        )
        bucket_hot = (tile_buckets[..., None] == bucket_range).astype(jnp.float32)
        lookup = jnp.einsum(
            "sijb,bh->shij", bucket_hot, bias_table, precision=lax.Precision.HIGHEST
        )
        raw_score = (
            raw_score
            + lookup
            + edge_slope[None, :, None, None] * tile_weights.astype(jnp.float32)[:, None]
        )
        row_max = jnp.max(raw_score, axis=-1)
        prob_vals = jnp.exp(raw_score - row_max[..., None]).astype(jnp.bfloat16)
        row_sum = jnp.sum(prob_vals.astype(jnp.float32), axis=-1)
        weighted = jnp.einsum(
            "shij,sjhd->sihd", prob_vals, value_sel, preferred_element_type=jnp.float32
        )
        return (row_max, row_sum, weighted)

    row_max, row_sum, weighted = lax.map(
        score_slots,
        (
            query_block.reshape(turn_count, batch_size),
            key_block.reshape(turn_count, batch_size),
            edge_values.reshape(turn_count, batch_size, tile_size, tile_size),
            bucket_tiles.reshape(turn_count, batch_size, tile_size, tile_size),
        ),
    )
    row_max = row_max.reshape(slot_count, head_count, tile_size)
    row_sum = row_sum.reshape(slot_count, head_count, tile_size)
    weighted = weighted.reshape(slot_count, tile_size, head_count, head_dim)
    member = query_block[None, :] == query_ids[:, None]
    chosen = member.astype(jnp.float32)
    block_max = jnp.max(jnp.where(member[:, :, None, None], row_max[None], LOW_FLOOR), axis=1)
    slot_max = jnp.einsum("qs,qhi->shi", chosen, block_max, precision=lax.Precision.HIGHEST)
    slot_live = (query_block >= 0)[:, None, None]
    factor = jnp.where(slot_live, jnp.exp(jnp.where(slot_live, row_max - slot_max, 0.0)), 0.0)
    block_sum = jnp.einsum("qs,shi->qih", chosen, factor * row_sum, precision=lax.Precision.HIGHEST)
    block_out = jnp.einsum(
        "qs,sihd->qihd",
        chosen,
        jnp.transpose(factor, (0, 2, 1))[..., None] * weighted,
        precision=lax.Precision.HIGHEST,
    )
    range_rows = query_count * tile_size
    max_rows = jnp.transpose(block_max, (0, 2, 1)).reshape(range_rows, head_count)
    sum_rows = block_sum.reshape(range_rows, head_count)
    out_rows = block_out.reshape(range_rows, head_count, head_dim)
    col_max, col_sum, col_out = (
        lax.all_to_all(max_rows[None], "col", split_axis=1, concat_axis=0, tiled=True),
        lax.all_to_all(sum_rows[None], "col", split_axis=1, concat_axis=0, tiled=True),
        lax.all_to_all(out_rows[None], "col", split_axis=1, concat_axis=0, tiled=True),
    )
    global_max = jnp.max(col_max, axis=0)
    col_factor = jnp.exp(col_max - global_max[None])
    mine_sum = jnp.sum(col_factor * col_sum, axis=0)
    mine_out = jnp.sum(col_factor[..., None] * col_out, axis=0)
    attention = (mine_out / mine_sum[..., None]).reshape(rows_own, model_width).astype(jnp.bfloat16)
    update = jnp.dot(attention, w_out, preferred_element_type=jnp.float32)
    return (node_features.astype(jnp.float32) + update).astype(jnp.bfloat16)


def solution(mesh):
    return jax.shard_map(
        local,
        mesh=mesh,
        in_specs=(
            P(("row", "col"), None),
            P(),
            P(),
            P(),
            P(),
            P(),
            P(),
            P("row", "col", None, None),
            P("row", "col", None, None, None),
            P("row", "col", None, None, None, None),
        ),
        out_specs=P(("row", "col"), None),
        check_vma=False,
    )
```

profile of v0, /device:TPU:0, one launch (start us, length us, event | category | flops | bytes accessed | tf_op | source)
XLA Modules:
  0.0 315.5 jit_solution(13089731285216129570)
XLA Ops:
  6.5 1.2 convert_reduce_fusion.1
  7.8 1.2 fusion.28
  9.0 3.9 %convolution_convert_fusion.2 = bf16[128,2048]{1,0:T(8,128)(2,1)} fusion(bf16[1024,2048]{1,0:T(8,128)(2,1)} %param.15, bf16[128,1024]{1,0:T(8,128)(2,1)} %param.12, f32[1024]{0:T(1024)} %param.13, f32[128]{0:T(128)S(1)} %add_rsqrt_fusion, f32[128]{0:T(128)S(1)} %broadcast_multiply_fusion), kind=kOutput, calls=%fused_computation.37 | convolution fusion | flops 537788416 | bytes 4985856 | tf_op jit(solution)/shard_map/dot_general | solution.py:38
  13.0 1.2 convolution_convert_fusion.3
  14.2 1.0 copy.100
  15.3 5.2 %all-to-all-start = ((bf16[1,1,4,4,128,128]{4,5,3,1,0,2:T(8,128)(2,1)}), bf16[1,1,4,4,128,128]{4,5,3,1,0,2:T(8,128)(2,1)}, u32[]{:S(2)}, u32[]{:S(2)}) async-start(bf16[1,1,4,4,128,128]{4,5,3,1,0,2:T(8,128)(2,1)} %copy.100), calls=%async_computation | async-start | bytes 1048576 | tf_op jit(solution)/shard_map/all_to_all | solution.py:42
  20.7 33.5 %all-gather.5.cloned.1.call-done = bf16[512,2048]{1,0:T(8,128)(2,1)} async-done(((bf16[128,2048]{1,0:T(8,128)(2,1)}), bf16[512,2048]{1,0:T(8,128)(2,1)}) %all-gather.5.cloned.1.call-update) | async-done | bytes 2097168 | tf_op jit(solution)/shard_map/all_gather | solution.py:41
  54.2 4.6 %reshape.131 = bf16[4,262144]{1,0:T(4,128)(2,1)} reshape(bf16[512,2048]{1,0:T(8,128)(2,1)} %all-gather.5.cloned.1.call-done) | data formatting | bytes 4194304 | tf_op jit(solution)/shard_map/reshape | solution.py:54
  58.8 26.2 %all-gather.3.cloned.1.call-done = bf16[1024,1024]{1,0:T(8,128)(2,1)} async-done(((bf16[128,1024]{1,0:T(8,128)(2,1)}), bf16[1024,1024]{1,0:T(8,128)(2,1)}) %all-gather.3.cloned.1.call-update) | async-done | bytes 2097168 | tf_op jit(solution)/shard_map/all_gather | solution.py:37
  85.0 3.8 %reshape.130 = bf16[8,131072]{1,0:T(8,128)(2,1)} reshape(bf16[1024,1024]{1,0:T(8,128)(2,1)} %all-gather.3.cloned.1.call-done) | data formatting | bytes 4194304 | tf_op jit(solution)/shard_map/reshape | solution.py:52
  88.8 80.2 %while.15 = (s32[]{:T(128)}, f32[4,4,8,128]{3,1,0,2:T(4,128)S(1)}, f32[4,4,8,128]{3,1,0,2:T(4,128)}, f32[4,4,128,8,128]{2,4,3,1,0:T(8,128)}, s32[4,4]{1,0:T(4,12...) while((s32[]{:T(128)}, f32[4,4,8,128]{3,1,0,2:T(4,128)S(1)}, ...), condition=%wide.region_5.6_spmd.clone, body=%wide.region_2.5_spmd.clone.sunk | while | flops 496033856 | bytes 54004036 | solution.py:99
  88.8 2.9 fusion.71
  92.0 1.4 fusion.72
  93.4 1.0 dynamic-slice_bitcast_fusion.2
  94.4 2.6 fusion.69
  97.0 1.9 copy.161
  98.8 2.5 fusion.74
  101.5 0.9 bitcast_convert_fusion.2
  102.5 0.9 fusion.75
  103.4 1.5 copy.164
  104.9 3.0 bitcast_dynamic-update-slice_fusion.2
  108.9 2.9 fusion.71
  112.1 1.4 fusion.72
  113.4 1.0 dynamic-slice_bitcast_fusion.2
  114.4 2.6 fusion.69
  117.0 1.9 copy.161
  118.9 2.5 fusion.74
  121.5 0.9 bitcast_convert_fusion.2
  122.5 0.9 fusion.75
  123.4 1.5 copy.164
  124.9 3.0 bitcast_dynamic-update-slice_fusion.2
  128.9 2.9 fusion.71
  132.1 1.4 fusion.72
  133.4 1.0 dynamic-slice_bitcast_fusion.2
  134.4 2.6 fusion.69
  137.0 1.9 copy.161
  138.9 2.5 fusion.74
  141.5 0.9 bitcast_convert_fusion.2
  142.5 0.9 fusion.75
  143.4 1.5 copy.164
  144.9 3.0 bitcast_dynamic-update-slice_fusion.2
  148.9 2.9 fusion.71
  152.1 1.4 fusion.72
  153.5 1.0 dynamic-slice_bitcast_fusion.2
  154.4 2.6 fusion.69
  157.0 1.9 copy.161
  158.9 2.5 fusion.74
  161.6 0.9 bitcast_convert_fusion.2
  162.5 0.9 fusion.75
  163.5 1.5 copy.164
  165.0 3.0 bitcast_dynamic-update-slice_fusion.2
  169.4 1.0 convolution_bitcast_fusion
  171.2 1.9 reduce.8
  173.1 0.9 reshape.155
  174.0 3.3 %all-to-all-start.3 = ((f32[8,1,1024]{2,1,0:T(1,128)}), f32[8,1,1024]{2,1,0:T(1,128)S(1)}, u32[]{:S(2)}, u32[]{:S(2)}) async-start(f32[8,1,1024]{2,1,0:T(1,128)} %reshape.155), calls=%async_computation.3 | async-start | bytes 65536 | tf_op jit(solution)/shard_map/all_to_all | solution.py:130
  177.7 1.9 reduce.10
  180.7 9.2 %copy.109 = f32[16,128,8,128]{3,0,2,1:T(8,128)} copy(f32[16,128,8,128]{1,3,2,0:T(8,128)} %bitcast.122) | data formatting | bytes 16777216 | tf_op jit(solution)/shard_map/reshape | solution.py:110
  189.9 5.0 %all-to-all-start.1 = ((f32[8,1,1024]{2,1,0:T(1,128)}), f32[8,1,1024]{2,1,0:T(1,128)S(1)}, u32[]{:S(2)}, u32[]{:S(2)}) async-start(f32[8,1,1024]{2,1,0:T(1,128)} %reshape.153), calls=%async_computation.1 | async-start | bytes 65536 | tf_op jit(solution)/shard_map/all_to_all | solution.py:129
  194.9 7.4 %fusion.19 = f32[8,128,8,128]{3,0,2,1:T(8,128)S(1)} fusion(f32[16,128,8,128]{3,0,2,1:T(8,128)} %copy.109, f32[16,128,8]{0,2,1:T(8,128)S(1)} %copy.108, s32[16]{0:T(128)S(1)} %get-tuple-element.149), kind=kOutput, calls=%fused_computation.33 | convolution fusion | flops 203423872 | bytes 12648512 | tf_op jit(solution)/shard_map/qs,sihd->qihd/dot_general | solution.py:118
  202.3 2.7 copy.110
  205.0 5.1 %all-to-all-start.2 = ((f32[1,1024,8,128]{3,2,0,1:T(8,128)}), f32[1,1024,8,128]{3,2,0,1:T(8,128)}, u32[]{:S(2)}, u32[]{:S(2)}) async-start(f32[1,1024,8,128]{3,2,0,1:T(8,128)} %bitcast.121), calls=%async_computation.2 | async-start | bytes 8388608 | tf_op jit(solution)/shard_map/all_to_all | solution.py:131
  214.0 90.2 %all-to-all-done.2 = f32[1,1024,8,128]{3,2,0,1:T(8,128)} async-done(((f32[1,1024,8,128]{3,2,0,1:T(8,128)}), f32[1,1024,8,128]{3,2,0,1:T(8,128)}, u32[]{:S(2)}, u32[]{:S(2)}) %all-to-all-start.2) | async-done | bytes 4194336 | tf_op jit(solution)/shard_map/all_to_all | solution.py:131
  304.2 3.0 multiply_reduce_fusion
  307.5 1.2 fusion.22
  (96 shorter events, 12.6 us)
Async XLA Ops:
  6.5 6.5 %copy-start = (bf16[1024,1024]{1,0:T(8,128)(2,1)S(1)}, bf16[1024,1024]{1,0:T(8,128)(2,1)}, u32[]{:S(2)}) copy-start(bf16[1024,1024]{1,0:T(8,128)(2,1)} %param.14) | copy-start | bytes 6291460
  6.5 47.6 %all-gather.5.cloned.1.call-start = ((), (), s32[]{:S(2)}) async-start(), calls=%async_computation.5 | async-start | bytes 2621440 | tf_op jit(solution)/shard_map/all_gather | solution.py:41
  8.9 4.1 %copy-start.4 = (bf16[128,1024]{1,0:T(8,128)(2,1)S(1)}, bf16[128,1024]{1,0:T(8,128)(2,1)}, u32[]{:S(2)}) copy-start(bf16[128,1024]{1,0:T(8,128)(2,1)} %param.12) | copy-start | bytes 786436
  9.0 4.1 %copy-start.8 = (f32[1024]{0:T(1024)S(1)}, f32[1024]{0:T(1024)}, u32[]{:S(2)}) copy-start(f32[1024]{0:T(1024)} %param.13) | copy-start | bytes 12292
  12.9 1.3 copy-start.6
  12.9 7.6 %copy-start.10 = (s32[1,1,2,16]{3,2,1,0:T(2,128)S(1)}, s32[1,1,2,16]{3,2,1,0:T(2,128)}, u32[]{:S(2)}) copy-start(s32[1,1,2,16]{3,2,1,0:T(2,128)} %param.19) | copy-start | bytes 388
  12.9 72.0 %all-gather.3.cloned.1.call-start = ((), (), s32[]{:S(2)}) async-start(), calls=%async_computation.4 | async-start | bytes 2359296 | tf_op jit(solution)/shard_map/all_gather | solution.py:37
  15.3 73.5 %all-to-all-start = ((bf16[1,1,4,4,128,128]{4,5,3,1,0,2:T(8,128)(2,1)}), bf16[1,1,4,4,128,128]{4,5,3,1,0,2:T(8,128)(2,1)}, u32[]{:S(2)}, u32[]{:S(2)}) async-start(bf16[1,1,4,4,128,128]{4,5,3,1,0,2:T(8,128)(2,1)} %copy.100), calls=%async_computation | async-start | bytes 1048576 | tf_op jit(solution)/shard_map/all_to_all | solution.py:42
  58.8 30.0 %copy-start.7 = (f32[32,8]{0,1:T(8,128)S(1)}, f32[32,8]{0,1:T(8,128)}, u32[]{:S(2)}) copy-start(f32[32,8]{0,1:T(8,128)} %param.17) | copy-start | bytes 3076
  58.8 30.0 %copy-start.9 = (f32[8]{0:T(128)S(1)}, f32[8]{0:T(128)}, u32[]{:S(2)}) copy-start(f32[8]{0:T(128)} %param.18) | copy-start | bytes 100
  98.8 3.6 %copy-start.2 = (f32[4,128,128,8]{1,2,3,0:T(8,128)S(1)}, f32[4,128,128,8]{1,2,3,0:T(8,128)}, u32[]{:S(2)}) copy-start(f32[4,128,128,8]{1,2,3,0:T(8,128)} %copy.161) | copy-start | bytes 6291460 | tf_op jit(solution)/shard_map/while
  98.8 3.6 %copy-start.3 = (bf16[4,128,1,8,128]{4,3,2,1,0:T(8,128)(2,1)S(1)}, bf16[4,128,1,8,128]{4,3,2,1,0:T(8,128)(2,1)}, u32[]{:S(2)}) copy-start(bf16[4,128,1,8,128]{4,3,2,1,0:T(8,128)(2,1)} %get-tuple-element.229) | copy-start | bytes 3145732 | tf_op jit(solution)/shard_map/while
  118.9 3.6 %copy-start.2 = (f32[4,128,128,8]{1,2,3,0:T(8,128)S(1)}, f32[4,128,128,8]{1,2,3,0:T(8,128)}, u32[]{:S(2)}) copy-start(f32[4,128,128,8]{1,2,3,0:T(8,128)} %copy.161) | copy-start | bytes 6291460 | tf_op jit(solution)/shard_map/while
  118.9 3.6 %copy-start.3 = (bf16[4,128,1,8,128]{4,3,2,1,0:T(8,128)(2,1)S(1)}, bf16[4,128,1,8,128]{4,3,2,1,0:T(8,128)(2,1)}, u32[]{:S(2)}) copy-start(bf16[4,128,1,8,128]{4,3,2,1,0:T(8,128)(2,1)} %get-tuple-element.229) | copy-start | bytes 3145732 | tf_op jit(solution)/shard_map/while
  138.9 3.6 %copy-start.2 = (f32[4,128,128,8]{1,2,3,0:T(8,128)S(1)}, f32[4,128,128,8]{1,2,3,0:T(8,128)}, u32[]{:S(2)}) copy-start(f32[4,128,128,8]{1,2,3,0:T(8,128)} %copy.161) | copy-start | bytes 6291460 | tf_op jit(solution)/shard_map/while
  138.9 3.6 %copy-start.3 = (bf16[4,128,1,8,128]{4,3,2,1,0:T(8,128)(2,1)S(1)}, bf16[4,128,1,8,128]{4,3,2,1,0:T(8,128)(2,1)}, u32[]{:S(2)}) copy-start(bf16[4,128,1,8,128]{4,3,2,1,0:T(8,128)(2,1)} %get-tuple-element.229) | copy-start | bytes 3145732 | tf_op jit(solution)/shard_map/while
  158.9 3.6 %copy-start.2 = (f32[4,128,128,8]{1,2,3,0:T(8,128)S(1)}, f32[4,128,128,8]{1,2,3,0:T(8,128)}, u32[]{:S(2)}) copy-start(f32[4,128,128,8]{1,2,3,0:T(8,128)} %copy.161) | copy-start | bytes 6291460 | tf_op jit(solution)/shard_map/while
  158.9 3.6 %copy-start.3 = (bf16[4,128,1,8,128]{4,3,2,1,0:T(8,128)(2,1)S(1)}, bf16[4,128,1,8,128]{4,3,2,1,0:T(8,128)(2,1)}, u32[]{:S(2)}) copy-start(bf16[4,128,1,8,128]{4,3,2,1,0:T(8,128)(2,1)} %get-tuple-element.229) | copy-start | bytes 3145732 | tf_op jit(solution)/shard_map/while
  174.0 15.9 %all-to-all-start.3 = ((f32[8,1,1024]{2,1,0:T(1,128)}), f32[8,1,1024]{2,1,0:T(1,128)S(1)}, u32[]{:S(2)}, u32[]{:S(2)}) async-start(f32[8,1,1024]{2,1,0:T(1,128)} %reshape.155), calls=%async_computation.3 | async-start | bytes 65536 | tf_op jit(solution)/shard_map/all_to_all | solution.py:130
  189.9 15.1 %all-to-all-start.1 = ((f32[8,1,1024]{2,1,0:T(1,128)}), f32[8,1,1024]{2,1,0:T(1,128)S(1)}, u32[]{:S(2)}, u32[]{:S(2)}) async-start(f32[8,1,1024]{2,1,0:T(1,128)} %reshape.153), calls=%async_computation.1 | async-start | bytes 65536 | tf_op jit(solution)/shard_map/all_to_all | solution.py:129
  205.0 99.2 %all-to-all-start.2 = ((f32[1,1024,8,128]{3,2,0,1:T(8,128)}), f32[1,1024,8,128]{3,2,0,1:T(8,128)}, u32[]{:S(2)}, u32[]{:S(2)}) async-start(f32[1,1024,8,128]{3,2,0,1:T(8,128)} %bitcast.121), calls=%async_computation.2 | async-start | bytes 8388608 | tf_op jit(solution)/shard_map/all_to_all | solution.py:131
  304.2 3.3 %copy-start.5 = (bf16[1024,1024]{1,0:T(8,128)(2,1)S(1)}, bf16[1024,1024]{1,0:T(8,128)(2,1)}, u32[]{:S(2)}) copy-start(bf16[1024,1024]{1,0:T(8,128)(2,1)} %param.16) | copy-start | bytes 6291460
  304.2 4.4 %copy-start.1 = (bf16[1024,1024]{1,0:T(8,128)(2,1)S(1)}, bf16[1024,1024]{1,0:T(8,128)(2,1)}, u32[]{:S(2)}) copy-start(bf16[1024,1024]{1,0:T(8,128)(2,1)} %param.14) | copy-start | bytes 6291460
Sparse Core Ops, SparseCore 0:
  13.0 41.0 all-gather.4
  55.8 29.1 all-gather.2
where the time goes:
time: 317 us; the launch traced here: 315 us
  waiting for transfers between devices  150 us (47%)
  matrix products  62.6 us (20%)
  local copies, waits for them, and re-layouts  54 us (17%)
  starting transfers between devices  18.7 us (6%)
  other arithmetic  16.3 us (5%)
  between operations  13.6 us (4%)
    all_to_all x1, waiting for transfers between devices, local(): lax.all_to_all(out_rows[None], 'col', split_axis=1, concat_axis=0, tiled=...  90.2 us
    all_gather x1, waiting for transfers between devices, local(): key_group = lax.all_gather(key_value, 'row', axis=0, tiled=True)  33.5 us
    all_gather x1, waiting for transfers between devices, local(): query_range = lax.all_gather(queries, 'col', axis=0, tiled=True)  26.2 us
    dot_general x4, matrix products, score_slots(): jnp.einsum('shij,sjhd->sihd', prob_vals, value_sel, preferred_element_typ...  12 us
    dot_general x4, matrix products, score_slots(): jnp.dot(key_pick, key_flat, preferred_element_type=jnp.float32)  11.5 us
    dot_general x4, matrix products, score_slots(): jnp.einsum('sijb,bh->shij', bucket_hot, bias_table, precision=lax.Precisi...  10.4 us
    dot_general x4, matrix products, score_slots(): jnp.dot(query_pick, query_flat, preferred_element_type=jnp.float32)  9.99 us
    reshape x1, local copies, waits for them, and re-layouts, local(): weighted = weighted.reshape(slot_count, tile_size, head_count, head_dim)  9.18 us
  transfers between devices with their start and end apart: 6, of which 3 were waited for; matrix products, arithmetic and copies ran while one was open for 12% of the time, Pallas kernels for 0%

commit v1 on v0

--- a/solution.py
+++ b/solution.py
@@ -38,7 +38,12 @@
     key_value = jnp.dot(normalized, w_keyvalue, preferred_element_type=jnp.float32).astype(
         jnp.bfloat16
     )
-    key_group = lax.all_gather(key_value, "row", axis=0, tiled=True)
+    ring = [key_value]
+    for hop in range(3):
+        ring.append(lax.ppermute(ring[-1], "row", [(dev, (dev + 1) % 4) for dev in range(4)]))
+    key_group = jnp.roll(
+        jnp.concatenate(ring[::-1], axis=0), (lax.axis_index("row") + 1) * ring[0].shape[0], axis=0
+    )
     arrived = lax.all_to_all(edge_weight, "row", split_axis=2, concat_axis=0, tiled=True)
     slot_count = arrived.shape[0] * arrived.shape[3]
     edge_values = arrived.reshape(slot_count, tile_size, tile_size)

time: 317 us -> 301 us (0.950)
  waiting for transfers between devices: 150 us -> 127 us
  starting transfers between devices: 18.7 us -> 22.4 us
    ppermute x0 -> x3, waiting for transfers between devices: none -> 37.1 us  [local(): lax.ppermute(ring[-1], 'row', [(dev, (dev + 1) % 4) for dev in range(4)])]
    all_gather x1 -> x0, waiting for transfers between devices: 33.5 us -> none  [local(): key_group = lax.all_gather(key_value, 'row', axis=0, tiled=True)]
    all_gather x1, waiting for transfers between devices: 26.2 us -> 0.01 us  [local(): query_range = lax.all_gather(queries, 'col', axis=0, tiled=True)]
    ppermute x0 -> x3, starting transfers between devices: none -> 3.8 us  [local(): lax.ppermute(ring[-1], 'row', [(dev, (dev + 1) % 4) for dev in range(4)])]
    unnamed x24 -> x29, local copies, waits for them, and re-layouts: 5.14 us -> 7.47 us
    while x28 -> x44, local copies, waits for them, and re-layouts: 7.73 us -> 7.76 us
  transfers between devices with their start and end apart: 6 -> 8, of which waited for: 3 -> 4; matrix products, arithmetic and copies ran while one was open for 12% -> 13% of each run, Pallas kernels for 0% -> 0%
where the time goes in v1:
time: 301 us; the launch traced here: 300 us
  waiting for transfers between devices  127 us (42%)
  matrix products  64.4 us (21%)
  local copies, waits for them, and re-layouts  55 us (18%)
  starting transfers between devices  22.4 us (7%)
  other arithmetic  16.3 us (5%)
  between operations  13.7 us (5%)
    all_to_all x1, waiting for transfers between devices, local(): lax.all_to_all(out_rows[None], 'col', split_axis=1, concat_axis=0, tiled=...  90.2 us
    ppermute x3, waiting for transfers between devices, local(): lax.ppermute(ring[-1], 'row', [(dev, (dev + 1) % 4) for dev in range(4)])  37.1 us
    dot_general x4, matrix products, score_slots(): jnp.dot(key_pick, key_flat, preferred_element_type=jnp.float32)  12.3 us
    dot_general x4, matrix products, score_slots(): jnp.einsum('shij,sjhd->sihd', prob_vals, value_sel, preferred_element_typ...  12.3 us
    dot_general x4, matrix products, score_slots(): jnp.einsum('sijb,bh->shij', bucket_hot, bias_table, precision=lax.Precisi...  10.4 us
    dot_general x4, matrix products, score_slots(): jnp.dot(query_pick, query_flat, preferred_element_type=jnp.float32)  9.99 us
    reshape x1, local copies, waits for them, and re-layouts, local(): weighted = weighted.reshape(slot_count, tile_size, head_count, head_dim)  9.18 us
    while x44, local copies, waits for them, and re-layouts  7.76 us
  transfers between devices with their start and end apart: 8, of which 4 were waited for; matrix products, arithmetic and copies ran while one was open for 13% of the time, Pallas kernels for 0%

profile of v1, /device:TPU:0, one launch (start us, length us, event | category | flops | bytes accessed | tf_op | source)
XLA Modules:
  0.0 299.6 jit_solution(17774593680715657817)
XLA Ops:
  6.6 1.2 convert_reduce_fusion.1
  7.8 1.2 fusion.28
  9.0 3.1 %convolution_convert_fusion.2 = bf16[128,2048]{1,0:T(8,128)(2,1)S(1)} fusion(bf16[1024,2048]{1,0:T(8,128)(2,1)} %param.15, bf16[128,1024]{1,0:T(8,128)(2,1)} %param.12, f32[1024]{0:T(1024)} %param.13, f32[128]{0:T(128)S(1)} %add_rsqrt_fusion, f32[128]{0:T(128)S(1)} %broadcast_multiply_fusion), kind=kOutput, calls=%fused_computation.37 | convolution fusion | flops 537788416 | bytes 4985856 | tf_op jit(solution)/shard_map/dot_general | solution.py:38
  12.1 3.0 %collective-permute-start = (bf16[128,2048]{1,0:T(8,128)(2,1)S(1)}, bf16[128,2048]{1,0:T(8,128)(2,1)}, u32[]{:S(2)}, u32[]{:S(2)}) collective-permute-start(bf16[128,2048]{1,0:T(8,128)(2,1)S(1)} %convolution_convert_fusion.2), channel_id=1, source_target_pairs={{0,8},{8,16},{16,24},{24,0},{1,9},{9,17},{17,25},{25,1},{2,10},{10... | collective-permute-start | bytes 1572872 | tf_op jit(solution)/shard_map/ppermute | solution.py:43
  15.1 1.2 convolution_convert_fusion.3
  16.4 11.8 %collective-permute-done = bf16[128,2048]{1,0:T(8,128)(2,1)} collective-permute-done((bf16[128,2048]{1,0:T(8,128)(2,1)S(1)}, bf16[128,2048]{1,0:T(8,128)(2,1)}, u32[]{:S(2)}, u32[]{:S(2)}) %collective-permute-start) | collective-permute-done | bytes 524320 | tf_op jit(solution)/shard_map/ppermute | solution.py:43
  28.9 1.0 copy.100
  29.9 3.7 %all-to-all-start = ((bf16[1,1,4,4,128,128]{4,5,3,1,0,2:T(8,128)(2,1)}), bf16[1,1,4,4,128,128]{4,5,3,1,0,2:T(8,128)(2,1)S(1)}, u32[]{:S(2)}, u32[]{:S(2)}) async-start(bf16[1,1,4,4,128,128]{4,5,3,1,0,2:T(8,128)(2,1)} %copy.100), calls=%async_computation | async-start | bytes 1048576 | tf_op jit(solution)/shard_map/all_to_all | solution.py:47
  33.6 10.5 %collective-permute-done.1 = bf16[128,2048]{1,0:T(8,128)(2,1)S(1)} collective-permute-done((bf16[128,2048]{1,0:T(8,128)(2,1)}, bf16[128,2048]{1,0:T(8,128)(2,1)S(1)}, u32[]{:S(2)}, u32[]{:S(2)}) %collective-permute-start.1) | collective-permute-done | bytes 524320 | tf_op jit(solution)/shard_map/ppermute | solution.py:43
  44.3 14.9 %collective-permute-done.2 = bf16[128,2048]{1,0:T(8,128)(2,1)S(1)} collective-permute-done((bf16[128,2048]{1,0:T(8,128)(2,1)S(1)}, bf16[128,2048]{1,0:T(8,128)(2,1)S(1)}, u32[]{:S(2)}, u32[]{:S(2)}) %collective-permute-start.2) | collective-permute-done | bytes 524320 | tf_op jit(solution)/shard_map/ppermute | solution.py:43
  59.3 1.1 constant_dynamic-update-slice_fusion.5
  60.5 1.1 constant_dynamic-update-slice_fusion.1
  61.8 2.9 reshape.131
  64.7 3.9 %reshape.130 = bf16[8,131072]{1,0:T(8,128)(2,1)} reshape(bf16[1024,1024]{1,0:T(8,128)(2,1)} %all-gather.2.cloned.1.call-done) | data formatting | bytes 4194304 | tf_op jit(solution)/shard_map/reshape | solution.py:57
  68.7 81.4 %while.15 = (s32[]{:T(128)}, f32[4,4,8,128]{3,1,0,2:T(4,128)S(1)}, f32[4,4,8,128]{3,1,0,2:T(4,128)}, f32[4,4,128,8,128]{2,4,3,1,0:T(8,128)}, s32[4,4]{1,0:T(4,12...) while((s32[]{:T(128)}, f32[4,4,8,128]{3,1,0,2:T(4,128)S(1)}, ...), condition=%wide.region_5.6_spmd.clone, body=%wide.region_2.5_spmd.clone.sunk | while | flops 496033856 | bytes 58198396 | solution.py:104
  68.9 3.1 %fusion.71 = bf16[1,4,2048,128]{3,1,2,0:T(4,128)(2,1)S(1)} fusion(bf16[4,262144]{1,0:T(4,128)(2,1)} %get-tuple-element.268, s32[4]{0:T(128)S(1)} %fusion.70), kind=kOutput, calls=%fused_computation.13.clone.1 | convolution fusion | flops 9437200 | bytes 4194320 | tf_op jit(solution)/shard_map/while/body/eval_jaxpr/dot_general | solution.py:77
  72.2 1.4 fusion.72
  73.6 1.0 dynamic-slice_bitcast_fusion.2
  74.6 2.6 fusion.69
  77.2 1.9 copy.161
  79.1 2.5 fusion.74
  81.7 0.9 bitcast_convert_fusion.2
  83.6 1.5 copy.164
  85.1 3.1 %bitcast_dynamic-update-slice_fusion.2 = f32[4,4,128,8,128]{2,4,3,1,0:T(8,128)} fusion(f32[4,4,128,8,128]{2,4,3,1,0:T(8,128)} %get-tuple-element.251, s32[]{:T(128)} %get-tuple-element.248, bf16[4,128,1,8,128]{1,4,3,0,2:T(8,128)(2,1)} %copy.164, f32[4,8,128,128]{2,3,1,0:T(8,128)S(1)} %get-tuple-element.230, f32[4,8,128]{2,1,0:T(8,128)S(1)} %get-tuple-element.231), kind=kOutput, calls=%fused_computation.8.clone.1 | convolution fusion | flops 135266304 | bytes 5259776 | tf_op jit(solution)/shard_map/while/body/eval_jaxpr/shij,sjhd->sihd/dot_general | solution.py:99
  89.2 3.1 %fusion.71 = bf16[1,4,2048,128]{3,1,2,0:T(4,128)(2,1)S(1)} fusion(bf16[4,262144]{1,0:T(4,128)(2,1)} %get-tuple-element.268, s32[4]{0:T(128)S(1)} %fusion.70), kind=kOutput, calls=%fused_computation.13.clone.1 | convolution fusion | flops 9437200 | bytes 4194320 | tf_op jit(solution)/shard_map/while/body/eval_jaxpr/dot_general | solution.py:77
  92.6 1.4 fusion.72
  93.9 1.0 dynamic-slice_bitcast_fusion.2
  94.9 2.6 fusion.69
  97.5 1.9 copy.161
  99.4 2.5 fusion.74
  102.0 0.9 bitcast_convert_fusion.2
  103.9 1.5 copy.164
  105.4 3.0 %bitcast_dynamic-update-slice_fusion.2 = f32[4,4,128,8,128]{2,4,3,1,0:T(8,128)} fusion(f32[4,4,128,8,128]{2,4,3,1,0:T(8,128)} %get-tuple-element.251, s32[]{:T(128)} %get-tuple-element.248, bf16[4,128,1,8,128]{1,4,3,0,2:T(8,128)(2,1)} %copy.164, f32[4,8,128,128]{2,3,1,0:T(8,128)S(1)} %get-tuple-element.230, f32[4,8,128]{2,1,0:T(8,128)S(1)} %get-tuple-element.231), kind=kOutput, calls=%fused_computation.8.clone.1 | convolution fusion | flops 135266304 | bytes 5259776 | tf_op jit(solution)/shard_map/while/body/eval_jaxpr/shij,sjhd->sihd/dot_general | solution.py:99
  109.4 3.1 %fusion.71 = bf16[1,4,2048,128]{3,1,2,0:T(4,128)(2,1)S(1)} fusion(bf16[4,262144]{1,0:T(4,128)(2,1)} %get-tuple-element.268, s32[4]{0:T(128)S(1)} %fusion.70), kind=kOutput, calls=%fused_computation.13.clone.1 | convolution fusion | flops 9437200 | bytes 4194320 | tf_op jit(solution)/shard_map/while/body/eval_jaxpr/dot_general | solution.py:77
  112.8 1.4 fusion.72
  114.2 1.0 dynamic-slice_bitcast_fusion.2
  115.1 2.6 fusion.69
  117.8 1.9 copy.161
  119.6 2.5 fusion.74
  122.3 0.9 bitcast_convert_fusion.2
  124.2 1.5 copy.164
  125.7 3.1 %bitcast_dynamic-update-slice_fusion.2 = f32[4,4,128,8,128]{2,4,3,1,0:T(8,128)} fusion(f32[4,4,128,8,128]{2,4,3,1,0:T(8,128)} %get-tuple-element.251, s32[]{:T(128)} %get-tuple-element.248, bf16[4,128,1,8,128]{1,4,3,0,2:T(8,128)(2,1)} %copy.164, f32[4,8,128,128]{2,3,1,0:T(8,128)S(1)} %get-tuple-element.230, f32[4,8,128]{2,1,0:T(8,128)S(1)} %get-tuple-element.231), kind=kOutput, calls=%fused_computation.8.clone.1 | convolution fusion | flops 135266304 | bytes 5259776 | tf_op jit(solution)/shard_map/while/body/eval_jaxpr/shij,sjhd->sihd/dot_general | solution.py:99
  129.7 3.1 %fusion.71 = bf16[1,4,2048,128]{3,1,2,0:T(4,128)(2,1)S(1)} fusion(bf16[4,262144]{1,0:T(4,128)(2,1)} %get-tuple-element.268, s32[4]{0:T(128)S(1)} %fusion.70), kind=kOutput, calls=%fused_computation.13.clone.1 | convolution fusion | flops 9437200 | bytes 4194320 | tf_op jit(solution)/shard_map/while/body/eval_jaxpr/dot_general | solution.py:77
  133.1 1.4 fusion.72
  134.5 1.0 dynamic-slice_bitcast_fusion.2
  135.5 2.6 fusion.69
  138.1 1.9 copy.161
  139.9 2.5 fusion.74
  142.6 0.9 bitcast_convert_fusion.2
  143.5 0.9 fusion.75
  144.5 1.5 copy.164
  146.0 3.1 %bitcast_dynamic-update-slice_fusion.2 = f32[4,4,128,8,128]{2,4,3,1,0:T(8,128)} fusion(f32[4,4,128,8,128]{2,4,3,1,0:T(8,128)} %get-tuple-element.251, s32[]{:T(128)} %get-tuple-element.248, bf16[4,128,1,8,128]{1,4,3,0,2:T(8,128)(2,1)} %copy.164, f32[4,8,128,128]{2,3,1,0:T(8,128)S(1)} %get-tuple-element.230, f32[4,8,128]{2,1,0:T(8,128)S(1)} %get-tuple-element.231), kind=kOutput, calls=%fused_computation.8.clone.1 | convolution fusion | flops 135266304 | bytes 5259776 | tf_op jit(solution)/shard_map/while/body/eval_jaxpr/shij,sjhd->sihd/dot_general | solution.py:99
  150.5 1.0 convolution_bitcast_fusion
  152.3 1.9 reduce.8
  155.1 4.8 %all-to-all-start.3 = ((f32[8,1,1024]{2,1,0:T(1,128)}), f32[8,1,1024]{2,1,0:T(1,128)S(1)}, u32[]{:S(2)}, u32[]{:S(2)}) async-start(f32[8,1,1024]{2,1,0:T(1,128)} %reshape.155), calls=%async_computation.3 | async-start | bytes 65536 | tf_op jit(solution)/shard_map/all_to_all | solution.py:135
  160.2 1.9 reduce.10
  163.2 9.2 %copy.109 = f32[16,128,8,128]{3,0,2,1:T(8,128)} copy(f32[16,128,8,128]{1,3,2,0:T(8,128)} %bitcast.122) | data formatting | bytes 16777216 | tf_op jit(solution)/shard_map/reshape | solution.py:115
  172.4 5.1 %all-to-all-start.1 = ((f32[8,1,1024]{2,1,0:T(1,128)}), f32[8,1,1024]{2,1,0:T(1,128)S(1)}, u32[]{:S(2)}, u32[]{:S(2)}) async-start(f32[8,1,1024]{2,1,0:T(1,128)} %reshape.153), calls=%async_computation.1 | async-start | bytes 65536 | tf_op jit(solution)/shard_map/all_to_all | solution.py:134
  177.5 7.4 %fusion.19 = f32[8,128,8,128]{3,0,2,1:T(8,128)S(1)} fusion(f32[16,128,8,128]{3,0,2,1:T(8,128)} %copy.109, f32[16,128,8]{0,2,1:T(8,128)S(1)} %copy.108, s32[16]{0:T(128)S(1)} %get-tuple-element.149), kind=kOutput, calls=%fused_computation.33 | convolution fusion | flops 203423872 | bytes 12648512 | tf_op jit(solution)/shard_map/qs,sihd->qihd/dot_general | solution.py:123
  184.9 2.7 copy.110
  187.6 5.1 %all-to-all-start.2 = ((f32[1,1024,8,128]{3,2,0,1:T(8,128)}), f32[1,1024,8,128]{3,2,0,1:T(8,128)}, u32[]{:S(2)}, u32[]{:S(2)}) async-start(f32[1,1024,8,128]{3,2,0,1:T(8,128)} %bitcast.121), calls=%async_computation.2 | async-start | bytes 8388608 | tf_op jit(solution)/shard_map/all_to_all | solution.py:136
  196.6 90.2 %all-to-all-done.2 = f32[1,1024,8,128]{3,2,0,1:T(8,128)} async-done(((f32[1,1024,8,128]{3,2,0,1:T(8,128)}), f32[1,1024,8,128]{3,2,0,1:T(8,128)}, u32[]{:S(2)}, u32[]{:S(2)}) %all-to-all-start.2) | async-done | bytes 4194336 | tf_op jit(solution)/shard_map/all_to_all | solution.py:136
  286.8 3.0 %multiply_reduce_fusion = f32[128,8,128]{2,1,0:T(8,128)S(1)} fusion(f32[8,128,8,128]{3,2,1,0:T(8,128)} %bitcast.14, f32[8,128,8]{2,1,0:T(8,128)S(1)} %copy.106), kind=kLoop, calls=%fused_computation.35 | loop fusion | flops 1966080 | bytes 4751360 | tf_op jit(solution)/shard_map/reduce_sum | solution.py:141
  290.0 2.7 fusion.22
  (122 shorter events, 17.4 us)
Async XLA Ops:
  6.5 8.6 %copy-start = (bf16[1024,1024]{1,0:T(8,128)(2,1)S(1)}, bf16[1024,1024]{1,0:T(8,128)(2,1)}, u32[]{:S(2)}) copy-start(bf16[1024,1024]{1,0:T(8,128)(2,1)} %param.14) | copy-start | bytes 6291460
  6.5 8.6 %copy-start.4 = (bf16[128,1024]{1,0:T(8,128)(2,1)S(1)}, bf16[128,1024]{1,0:T(8,128)(2,1)}, u32[]{:S(2)}) copy-start(bf16[128,1024]{1,0:T(8,128)(2,1)} %param.12) | copy-start | bytes 786436
  6.5 8.6 %copy-start.9 = (f32[1024]{0:T(1024)S(1)}, f32[1024]{0:T(1024)}, u32[]{:S(2)}) copy-start(f32[1024]{0:T(1024)} %param.13) | copy-start | bytes 12292
  6.5 22.3 %copy-start.7 = (bf16[1,1,4,4,128,128]{5,4,3,2,1,0:T(8,128)(2,1)S(1)}, bf16[1,1,4,4,128,128]{5,4,3,2,1,0:T(8,128)(2,1)}, u32[]{:S(2)}) copy-start(bf16[1,1,4,4,128,128]{5,4,3,2,1,0:T(8,128)(2,1)} %param.21) | copy-start | bytes 1572868
  6.5 58.2 %all-gather.2.cloned.1.call-start = ((), (), s32[]{:S(2)}) async-start(), calls=%async_computation.4 | async-start | bytes 2359296 | tf_op jit(solution)/shard_map/all_gather | solution.py:37
  9.0 24.6 %copy-start.11 = (s32[1,1,2,16]{3,2,1,0:T(2,128)S(1)}, s32[1,1,2,16]{3,2,1,0:T(2,128)}, u32[]{:S(2)}) copy-start(s32[1,1,2,16]{3,2,1,0:T(2,128)} %param.19) | copy-start | bytes 388
  12.1 16.0 %collective-permute-start = (bf16[128,2048]{1,0:T(8,128)(2,1)S(1)}, bf16[128,2048]{1,0:T(8,128)(2,1)}, u32[]{:S(2)}, u32[]{:S(2)}) collective-permute-start(bf16[128,2048]{1,0:T(8,128)(2,1)S(1)} %convolution_convert_fusion.2), channel_id=1, source_target_pairs={{0,8},{8,16},{16,24},{24,0},{1,9},{9,17},{17,25},{25,1},{2,10},{10... | collective-permute-start | bytes 1572872 | tf_op jit(solution)/shard_map/ppermute | solution.py:43
  28.1 15.9 %collective-permute-start.1 = (bf16[128,2048]{1,0:T(8,128)(2,1)}, bf16[128,2048]{1,0:T(8,128)(2,1)S(1)}, u32[]{:S(2)}, u32[]{:S(2)}) collective-permute-start(bf16[128,2048]{1,0:T(8,128)(2,1)} %collective-permute-done), channel_id=1, source_target_pairs={{0,8},{8,16},{16,24},{24,0},{1,9},{9,17},{17,25},{25,1},{2,10},{10... | collective-permute-start | bytes 1572872 | tf_op jit(solution)/shard_map/ppermute | solution.py:43
  29.9 38.7 %all-to-all-start = ((bf16[1,1,4,4,128,128]{4,5,3,1,0,2:T(8,128)(2,1)}), bf16[1,1,4,4,128,128]{4,5,3,1,0,2:T(8,128)(2,1)S(1)}, u32[]{:S(2)}, u32[]{:S(2)}) async-start(bf16[1,1,4,4,128,128]{4,5,3,1,0,2:T(8,128)(2,1)} %copy.100), calls=%async_computation | async-start | bytes 1048576 | tf_op jit(solution)/shard_map/all_to_all | solution.py:47
  44.1 15.1 %collective-permute-start.2 = (bf16[128,2048]{1,0:T(8,128)(2,1)S(1)}, bf16[128,2048]{1,0:T(8,128)(2,1)S(1)}, u32[]{:S(2)}, u32[]{:S(2)}) collective-permute-start(bf16[128,2048]{1,0:T(8,128)(2,1)S(1)} %collective-permute-done.1), channel_id=1, source_target_pairs={{0,8},{8,16},{16,24},{24,0},{1,9},{9,17},{17,25},{25,1},{2,10},{10... | collective-permute-start | bytes 1572872 | tf_op jit(solution)/shard_map/ppermute | solution.py:43
  61.8 6.9 %copy-start.8 = (f32[32,8]{0,1:T(8,128)S(1)}, f32[32,8]{0,1:T(8,128)}, u32[]{:S(2)}) copy-start(f32[32,8]{0,1:T(8,128)} %param.17) | copy-start | bytes 3076
  61.8 6.9 %copy-start.10 = (f32[8]{0:T(128)S(1)}, f32[8]{0:T(128)}, u32[]{:S(2)}) copy-start(f32[8]{0:T(128)} %param.18) | copy-start | bytes 100
  68.9 3.4 %copy-start.5 = (bf16[4,4,128,128]{2,3,1,0:T(8,128)(2,1)}, bf16[4,4,128,128]{2,3,1,0:T(8,128)(2,1)S(1)}, u32[]{:S(2)}) copy-start(bf16[4,4,128,128]{2,3,1,0:T(8,128)(2,1)S(1)} %get-tuple-element.272) | copy-start | bytes 1572868 | tf_op jit(solution)/shard_map/while
  79.1 3.6 %copy-start.2 = (f32[4,128,128,8]{1,2,3,0:T(8,128)S(1)}, f32[4,128,128,8]{1,2,3,0:T(8,128)}, u32[]{:S(2)}) copy-start(f32[4,128,128,8]{1,2,3,0:T(8,128)} %copy.161) | copy-start | bytes 6291460 | tf_op jit(solution)/shard_map/while
  79.1 3.6 %copy-start.3 = (bf16[4,128,1,8,128]{4,3,2,1,0:T(8,128)(2,1)S(1)}, bf16[4,128,1,8,128]{4,3,2,1,0:T(8,128)(2,1)}, u32[]{:S(2)}) copy-start(bf16[4,128,1,8,128]{4,3,2,1,0:T(8,128)(2,1)} %get-tuple-element.229) | copy-start | bytes 3145732 | tf_op jit(solution)/shard_map/while
  85.1 4.1 %copy-start.6 = (bf16[4,4,128,128]{2,3,1,0:T(8,128)(2,1)S(1)}, bf16[4,4,128,128]{2,3,1,0:T(8,128)(2,1)}, u32[]{:S(2)}) copy-start(bf16[4,4,128,128]{2,3,1,0:T(8,128)(2,1)} %copy-done.5) | copy-start | bytes 1572868 | tf_op jit(solution)/shard_map/while
  89.2 3.4 %copy-start.5 = (bf16[4,4,128,128]{2,3,1,0:T(8,128)(2,1)}, bf16[4,4,128,128]{2,3,1,0:T(8,128)(2,1)S(1)}, u32[]{:S(2)}) copy-start(bf16[4,4,128,128]{2,3,1,0:T(8,128)(2,1)S(1)} %get-tuple-element.272) | copy-start | bytes 1572868 | tf_op jit(solution)/shard_map/while
  99.4 3.6 %copy-start.2 = (f32[4,128,128,8]{1,2,3,0:T(8,128)S(1)}, f32[4,128,128,8]{1,2,3,0:T(8,128)}, u32[]{:S(2)}) copy-start(f32[4,128,128,8]{1,2,3,0:T(8,128)} %copy.161) | copy-start | bytes 6291460 | tf_op jit(solution)/shard_map/while
  99.4 3.6 %copy-start.3 = (bf16[4,128,1,8,128]{4,3,2,1,0:T(8,128)(2,1)S(1)}, bf16[4,128,1,8,128]{4,3,2,1,0:T(8,128)(2,1)}, u32[]{:S(2)}) copy-start(bf16[4,128,1,8,128]{4,3,2,1,0:T(8,128)(2,1)} %get-tuple-element.229) | copy-start | bytes 3145732 | tf_op jit(solution)/shard_map/while
  105.4 4.0 %copy-start.6 = (bf16[4,4,128,128]{2,3,1,0:T(8,128)(2,1)S(1)}, bf16[4,4,128,128]{2,3,1,0:T(8,128)(2,1)}, u32[]{:S(2)}) copy-start(bf16[4,4,128,128]{2,3,1,0:T(8,128)(2,1)} %copy-done.5) | copy-start | bytes 1572868 | tf_op jit(solution)/shard_map/while
  109.4 3.4 %copy-start.5 = (bf16[4,4,128,128]{2,3,1,0:T(8,128)(2,1)}, bf16[4,4,128,128]{2,3,1,0:T(8,128)(2,1)S(1)}, u32[]{:S(2)}) copy-start(bf16[4,4,128,128]{2,3,1,0:T(8,128)(2,1)S(1)} %get-tuple-element.272) | copy-start | bytes 1572868 | tf_op jit(solution)/shard_map/while
  119.6 3.6 %copy-start.2 = (f32[4,128,128,8]{1,2,3,0:T(8,128)S(1)}, f32[4,128,128,8]{1,2,3,0:T(8,128)}, u32[]{:S(2)}) copy-start(f32[4,128,128,8]{1,2,3,0:T(8,128)} %copy.161) | copy-start | bytes 6291460 | tf_op jit(solution)/shard_map/while
  119.6 3.6 %copy-start.3 = (bf16[4,128,1,8,128]{4,3,2,1,0:T(8,128)(2,1)S(1)}, bf16[4,128,1,8,128]{4,3,2,1,0:T(8,128)(2,1)}, u32[]{:S(2)}) copy-start(bf16[4,128,1,8,128]{4,3,2,1,0:T(8,128)(2,1)} %get-tuple-element.229) | copy-start | bytes 3145732 | tf_op jit(solution)/shard_map/while
  125.7 4.1 %copy-start.6 = (bf16[4,4,128,128]{2,3,1,0:T(8,128)(2,1)S(1)}, bf16[4,4,128,128]{2,3,1,0:T(8,128)(2,1)}, u32[]{:S(2)}) copy-start(bf16[4,4,128,128]{2,3,1,0:T(8,128)(2,1)} %copy-done.5) | copy-start | bytes 1572868 | tf_op jit(solution)/shard_map/while
  129.7 3.4 %copy-start.5 = (bf16[4,4,128,128]{2,3,1,0:T(8,128)(2,1)}, bf16[4,4,128,128]{2,3,1,0:T(8,128)(2,1)S(1)}, u32[]{:S(2)}) copy-start(bf16[4,4,128,128]{2,3,1,0:T(8,128)(2,1)S(1)} %get-tuple-element.272) | copy-start | bytes 1572868 | tf_op jit(solution)/shard_map/while
  139.9 3.6 %copy-start.2 = (f32[4,128,128,8]{1,2,3,0:T(8,128)S(1)}, f32[4,128,128,8]{1,2,3,0:T(8,128)}, u32[]{:S(2)}) copy-start(f32[4,128,128,8]{1,2,3,0:T(8,128)} %copy.161) | copy-start | bytes 6291460 | tf_op jit(solution)/shard_map/while
  139.9 3.6 %copy-start.3 = (bf16[4,128,1,8,128]{4,3,2,1,0:T(8,128)(2,1)S(1)}, bf16[4,128,1,8,128]{4,3,2,1,0:T(8,128)(2,1)}, u32[]{:S(2)}) copy-start(bf16[4,128,1,8,128]{4,3,2,1,0:T(8,128)(2,1)} %get-tuple-element.229) | copy-start | bytes 3145732 | tf_op jit(solution)/shard_map/while
  146.0 4.1 %copy-start.6 = (bf16[4,4,128,128]{2,3,1,0:T(8,128)(2,1)S(1)}, bf16[4,4,128,128]{2,3,1,0:T(8,128)(2,1)}, u32[]{:S(2)}) copy-start(bf16[4,4,128,128]{2,3,1,0:T(8,128)(2,1)} %copy-done.5) | copy-start | bytes 1572868 | tf_op jit(solution)/shard_map/while
  155.1 17.3 %all-to-all-start.3 = ((f32[8,1,1024]{2,1,0:T(1,128)}), f32[8,1,1024]{2,1,0:T(1,128)S(1)}, u32[]{:S(2)}, u32[]{:S(2)}) async-start(f32[8,1,1024]{2,1,0:T(1,128)} %reshape.155), calls=%async_computation.3 | async-start | bytes 65536 | tf_op jit(solution)/shard_map/all_to_all | solution.py:135
  172.4 15.2 %all-to-all-start.1 = ((f32[8,1,1024]{2,1,0:T(1,128)}), f32[8,1,1024]{2,1,0:T(1,128)S(1)}, u32[]{:S(2)}, u32[]{:S(2)}) async-start(f32[8,1,1024]{2,1,0:T(1,128)} %reshape.153), calls=%async_computation.1 | async-start | bytes 65536 | tf_op jit(solution)/shard_map/all_to_all | solution.py:134
  187.6 99.2 %all-to-all-start.2 = ((f32[1,1024,8,128]{3,2,0,1:T(8,128)}), f32[1,1024,8,128]{3,2,0,1:T(8,128)}, u32[]{:S(2)}, u32[]{:S(2)}) async-start(f32[1,1024,8,128]{3,2,0,1:T(8,128)} %bitcast.121), calls=%async_computation.2 | async-start | bytes 8388608 | tf_op jit(solution)/shard_map/all_to_all | solution.py:136
  286.8 6.0 %copy-start.1 = (bf16[1024,1024]{1,0:T(8,128)(2,1)S(1)}, bf16[1024,1024]{1,0:T(8,128)(2,1)}, u32[]{:S(2)}) copy-start(bf16[1024,1024]{1,0:T(8,128)(2,1)} %param.14) | copy-start | bytes 6291460
Sparse Core Ops, SparseCore 0:
  16.5 29.4 all-gather.1
